TPU v7x, 256 devices: a whole 4x4x8 slice. The times are simulated.
256 devices in a mesh: seq: 32 (over z, y), mp: 8 (over x, core).
Axes of the slice: x: 4, y: 4, z: 8, core: 2. Of those that a mesh axis runs over, the one named last changes fastest.
Arguments:
- tokens: bfloat16 [12288, 4096], P('seq', 'mp'), may hold values from -6 to 6
- norm_gain: float32 [2, 4096], replicated, may hold values from 0.25 to 1.75
- in_weight: bfloat16 [2, 3, 4096, 4096], P(None, None, 'seq', 'mp'), may hold values from -0.09375 to 0.09375
- feat_filter: float32 [2, 3, 3, 4096], P(None, None, None, 'mp'), may hold values from -3 to 3
- short_filter: float32 [256, 7], P('mp'), may hold values from -3 to 3
- medium_filter: float32 [256, 128], P('mp'), may hold values from -0.4 to 0.4
- out_weight: bfloat16 [4096, 4096], P('seq', 'mp'), may hold values from -0.09375 to 0.09375
Outputs:
- stream: bfloat16 [12288, 4096], P('seq', 'mp')
- mixed: bfloat16 [12288, 4096], P('seq', 'mp')
All inputs are finite; a program needn't handle non-finite values.
Results may differ from a plain program's by a relative error of at most 0.015.
Values may be sent and summed in bfloat16 or wider, within the bound.
A program may use at most 128 MiB of HBM per device.

v0:
```python
import jax
import jax.numpy as jnp
from jax import lax
from jax.sharding import PartitionSpec as P


def shifted(x, axis, by):
    peers = lax.axis_size(axis)
    pairs = [(i, i + by) for i in range(peers) if 0 <= i + by < peers]
    return lax.ppermute(x, axis, pairs)


def causal_taps(extended, taps, count):
    reach = taps.shape[0] - 1
    offset = extended.shape[0] - count - reach
    values = extended.astype(jnp.float32)
    total = jnp.zeros((count, extended.shape[1]), jnp.float32)
    for index in range(reach + 1):
        begin = offset + reach - index
        total = total + taps[index] * values[begin : begin + count]
    return total


def toeplitz_conv(kv_ext, filt, count):
    width = filt.shape[1]
    channels = kv_ext.shape[1]
    groups_here = filt.shape[0]
    per_group = channels // groups_here
    padded = jnp.concatenate([jnp.zeros((1, channels), kv_ext.dtype), kv_ext], axis=0)
    blocks = padded.astype(jnp.float32).reshape(count // width + 1, width, groups_here, per_group)
    lag = jnp.arange(width)[:, None] - jnp.arange(width)[None, :]
    current = jnp.where(lag >= 0, filt[:, jnp.clip(lag, 0, width - 1)], 0.0)
    earlier = jnp.where(lag < 0, filt[:, jnp.clip(lag + width, 0, width - 1)], 0.0)
    out = jnp.einsum("gik,bkgc->bigc", current, blocks[1:], precision=lax.Precision.HIGHEST)
    out = out + jnp.einsum("gik,bkgc->bigc", earlier, blocks[:-1], precision=lax.Precision.HIGHEST)
    return out.reshape(count, channels)


def normalized(stream_loc, gain):
    full = lax.all_gather(stream_loc, "mp", axis=1, tiled=True)
    values = full.astype(jnp.float32)
    mean_sq = jnp.mean(values * values, axis=-1, keepdims=True)
    return (values * lax.rsqrt(mean_sq + 1e-06) * gain).astype(jnp.bfloat16)


def project(normed, weights):
    return jnp.einsum(
        "rd,cdf->crf",
        normed,
        lax.all_gather(weights, "seq", axis=1, tiled=True),
        preferred_element_type=jnp.float32,
    ).astype(jnp.bfloat16)


def gated_mix(proj, feat_taps, inner_fn, span):
    rows = proj.shape[1]
    reach = feat_taps.shape[1] - 1
    rim = shifted(proj[:, rows - reach :, :], "seq", 1)
    extended = jnp.concatenate([rim, proj], axis=1)
    query = causal_taps(extended[0], feat_taps[0], rows)
    key_part = causal_taps(extended[1], feat_taps[1], rows)
    value_part = causal_taps(extended[2], feat_taps[2], rows)
    kv_prod = (key_part * value_part).astype(jnp.bfloat16)
    earlier = shifted(kv_prod[rows - span :], "seq", 1)
    kv_ext = jnp.concatenate([earlier, kv_prod], axis=0)
    inner = inner_fn(kv_ext, rows)
    return (query * inner).astype(jnp.bfloat16)


def local(tokens, norm_gain, in_weight, feat_filter, short_filter, medium_filter, out_weight):
    per_group = tokens.shape[1] // short_filter.shape[0]
    short_taps = jnp.repeat(short_filter.T, per_group, axis=1)

    def short_inner(kv_ext, count):
        return causal_taps(kv_ext, short_taps, count)

    def medium_inner(kv_ext, count):
        return toeplitz_conv(kv_ext, medium_filter, count)

    normed = normalized(tokens, norm_gain[0])
    proj = project(normed, in_weight[0])
    first = gated_mix(proj, feat_filter[0], short_inner, short_filter.shape[1] - 1)
    first_full = lax.all_gather(first, "mp", axis=1, tiled=True)
    delta = jnp.dot(
        first_full,
        lax.all_gather(out_weight, "seq", axis=0, tiled=True),
        preferred_element_type=jnp.float32,
    )
    stream = (tokens.astype(jnp.float32) + delta).astype(jnp.bfloat16)
    normed_next = normalized(stream, norm_gain[1])
    proj_next = project(normed_next, in_weight[1])
    mixed = gated_mix(proj_next, feat_filter[1], medium_inner, medium_filter.shape[1] - 1)
    return (stream, mixed)


def solution(mesh):
    placed = (
        P("seq", "mp"),
        P(),
        P(None, None, "seq", "mp"),
        P(None, None, None, "mp"),
        P("mp", None),
        P("mp", None),
        P("seq", "mp"),
    )
    return jax.shard_map(
        local,
        mesh=mesh,
        in_specs=placed,
        out_specs=(P("seq", "mp"), P("seq", "mp")),
        check_vma=False,
    )
```

profile of v0, /device:TPU:88, one launch (start us, length us, event | category | flops | bytes accessed | tf_op | source)
XLA Modules:
  0.0 597.8 jit_solution(11730328731184018714)
XLA Ops:
  7.2 0.7 all-gather.9.cloned.1.call-update
  7.9 2.1 fusion.119
  10.1 0.7 all-gather.13.cloned.1.call-update
  10.8 0.9 fusion.121
  11.7 30.4 %all-gather.9.cloned.1.call-done = bf16[384,4096]{1,0:T(8,128)(2,1)} async-done(((bf16[384,512]{1,0:T(8,128)(2,1)}), bf16[384,4096]{1,0:T(8,128)(2,1)}) %all-gather.9.cloned.1.call-update) | async-done | bytes 3145744 | tf_op jit(solution)/shard_map/all_gather | solution.py:40
  42.1 2.7 fusion.4
  44.9 116.5 %all-gather.17.cloned.1.call-done = bf16[1,3,4096,512]{3,2,1,0:T(8,128)(2,1)} async-done(((bf16[1,3,128,512]{3,2,1,0:T(8,128)(2,1)}), bf16[1,3,4096,512]{3,2,1,0:T(8,128)(2,1)}) %all-gather.17.cloned.1.call-update) | async-done | bytes 12582928 | tf_op jit(solution)/shard_map/all_gather | solution.py:50
  161.4 8.3 %fusion.39 = bf16[3,384,512]{2,1,0:T(8,128)(2,1)S(1)} fusion(bf16[1,3,4096,512]{3,2,1,0:T(8,128)(2,1)} %all-gather.17.cloned.1.call-done, bf16[384,4096]{1,0:T(8,128)(2,1)S(1)} %copy-done.1, f32[4096]{0:T(1024)S(1)} %bitcast.255, f32[384]{0:T(512)S(1)} %add_rsqrt_fusion.1), kind=kOutput, calls=%fused_computation.35 | convolution fusion | flops 4838719488 | bytes 16926208 | tf_op jit(solution)/shard_map/rd,cdf->crf/dot_general | solution.py:47
  169.7 6.5 %collective-permute-start = (bf16[3,2,512]{2,1,0:T(2,128)(2,1)S(1)}, bf16[3,2,512]{2,1,0:T(2,128)(2,1)S(1)}, u32[]{:S(2)}, u32[]{:S(2)}) collective-permute-start(bf16[3,2,512]{2,1,0:T(2,128)(2,1)S(1)} %slice.436), channel_id=1, source_target_pairs={{0,8},{8,16},{16,24},{24,32},{32,40},{40,48},{48,56},{56,64},{64,7... | collective-permute-start | bytes 18440 | tf_op jit(solution)/shard_map/ppermute | solution.py:10
  176.2 0.6 fusion.120
  176.8 0.7 collective-permute-done
  177.5 0.3 fusion.106
  177.8 0.5 fusion.85
  178.3 6.3 %collective-permute-start.1 = (bf16[6,512]{1,0:T(8,128)(2,1)S(1)}, bf16[6,512]{1,0:T(8,128)(2,1)S(1)}, u32[]{:S(2)}, u32[]{:S(2)}) collective-permute-start(bf16[6,512]{1,0:T(8,128)(2,1)S(1)} %slice.450), channel_id=1, source_target_pairs={{0,8},{8,16},{16,24},{24,32},{32,40},{40,48},{48,56},{56,64},{64,7... | collective-permute-start | bytes 18440 | tf_op jit(solution)/shard_map/ppermute | solution.py:10
  184.8 0.1 broadcast_in_dim.51
  185.3 0.1 broadcast_in_dim.58
  185.8 0.2 collective-permute-done.1
  186.0 0.1 maximum_convert_fusion
  186.1 1.7 fusion.76
  187.9 55.7 %all-gather.13.cloned.1.call-done = bf16[4096,512]{1,0:T(8,128)(2,1)} async-done(((bf16[128,512]{1,0:T(8,128)(2,1)}), bf16[4096,512]{1,0:T(8,128)(2,1)}) %all-gather.13.cloned.1.call-update) | async-done | bytes 4194320 | tf_op jit(solution)/shard_map/all_gather | solution.py:86
  243.6 32.9 %all-gather.11.cloned.1.call-done = bf16[384,4096]{1,0:T(8,128)(2,1)} async-done(((bf16[384,512]{1,0:T(8,128)(2,1)}), bf16[384,4096]{1,0:T(8,128)(2,1)}) %all-gather.11.cloned.1.call-update) | async-done | bytes 3145744 | tf_op jit(solution)/shard_map/all_gather | solution.py:83
  276.5 5.7 fusion.50
  282.2 0.5 all-gather.19.cloned.1.call-update
  282.8 29.9 %all-gather.15.cloned.1.call-done = bf16[384,4096]{1,0:T(8,128)(2,1)} async-done(((bf16[384,512]{1,0:T(8,128)(2,1)}), bf16[384,4096]{1,0:T(8,128)(2,1)}) %all-gather.15.cloned.1.call-update) | async-done | bytes 3145744 | tf_op jit(solution)/shard_map/all_gather | solution.py:40
  312.7 2.7 fusion.7
  315.4 116.4 %all-gather.19.cloned.1.call-done = bf16[1,3,4096,512]{3,2,1,0:T(8,128)(2,1)} async-done(((bf16[1,3,128,512]{3,2,1,0:T(8,128)(2,1)}), bf16[1,3,4096,512]{3,2,1,0:T(8,128)(2,1)}) %all-gather.19.cloned.1.call-update) | async-done | bytes 12582928 | tf_op jit(solution)/shard_map/all_gather | solution.py:50
  431.8 8.2 %fusion.34 = bf16[3,384,512]{2,1,0:T(8,128)(2,1)S(1)} fusion(bf16[1,3,4096,512]{3,2,1,0:T(8,128)(2,1)} %all-gather.19.cloned.1.call-done, bf16[384,4096]{1,0:T(8,128)(2,1)S(1)} %copy-done.2, f32[4096]{0:T(1024)S(1)} %bitcast.254, f32[384]{0:T(512)S(1)} %add_rsqrt_fusion), kind=kOutput, calls=%fused_computation.34 | convolution fusion | flops 4838719488 | bytes 16926208 | tf_op jit(solution)/shard_map/rd,cdf->crf/dot_general | solution.py:47
  440.1 6.5 %collective-permute-start.2 = (bf16[3,2,512]{2,1,0:T(2,128)(2,1)S(1)}, bf16[3,2,512]{2,1,0:T(2,128)(2,1)S(1)}, u32[]{:S(2)}, u32[]{:S(2)}) collective-permute-start(bf16[3,2,512]{2,1,0:T(2,128)(2,1)S(1)} %slice.458), channel_id=1, source_target_pairs={{0,8},{8,16},{16,24},{24,32},{32,40},{40,48},{48,56},{56,64},{64,7... | collective-permute-start | bytes 18440 | tf_op jit(solution)/shard_map/ppermute | solution.py:10
  446.7 1.3 collective-permute-done.2
  447.9 0.3 fusion.102
  448.2 0.5 fusion.58
  448.8 6.5 %collective-permute-start.3 = (bf16[127,512]{1,0:T(8,128)(2,1)S(1)}, bf16[127,512]{1,0:T(8,128)(2,1)}, u32[]{:S(2)}, u32[]{:S(2)}) collective-permute-start(bf16[127,512]{1,0:T(8,128)(2,1)S(1)} %slice.472), channel_id=1, source_target_pairs={{0,8},{8,16},{16,24},{24,32},{32,40},{40,48},{48,56},{56,64},{64,7... | collective-permute-start | bytes 390152 | tf_op jit(solution)/shard_map/ppermute | solution.py:10
  455.3 0.6 fusion.115
  455.9 0.1 copy.17
  456.0 54.8 %gather_fusion.1 = f32[16384,32]{1,0:T(8,128)} fusion(f32[32,128]{0,1:T(8,128)S(1)} %copy.17, s32[16384]{0:T(1024)S(1)} %fusion.114), kind=kCustom, calls=%fused_computation.1 | custom fusion | bytes 4259840 | tf_op jit(solution)/shard_map/gather | solution.py:33
  510.8 5.5 copy.22
  516.3 54.8 %gather_fusion = f32[16384,32]{1,0:T(8,128)} fusion(f32[32,128]{0,1:T(8,128)S(1)} %copy.17, s32[16384]{0:T(1024)S(1)} %fusion.112), kind=kCustom, calls=%fused_computation | custom fusion | bytes 4259840 | tf_op jit(solution)/shard_map/gather | solution.py:32
  571.1 6.4 %copy.18 = f32[128,128,32]{1,0,2:T(8,128)} copy(f32[128,128,32]{2,1,0:T(8,128)} %bitcast.250) | data formatting | bytes 4194304 | tf_op jit(solution)/shard_map/gather | solution.py:32
  577.5 0.9 copy.16
  578.4 2.0 slice.428
  580.5 1.8 pad_maximum_fusion.2
  582.3 1.2 copy.20
  583.5 0.9 slice.431
  584.4 2.9 fusion.18
  587.4 1.8 fusion.47
  589.2 0.4 copy.24
  589.7 0.3 copy.25
  590.0 1.0 fusion.70
  (58 shorter events, 1.5 us)
Async XLA Ops:
  7.2 35.0 %all-gather.9.cloned.1.call-start = ((), (), s32[]{:S(2)}) async-start(), calls=%async_computation | async-start | bytes 3538944 | tf_op jit(solution)/shard_map/all_gather | solution.py:40
  7.9 153.5 %all-gather.17.cloned.1.call-start = ((), (), s32[]{:S(2)}) async-start(), calls=%async_computation.4 | async-start | bytes 12976128 | tf_op jit(solution)/shard_map/all_gather | solution.py:50
  10.0 233.5 %all-gather.13.cloned.1.call-start = ((), (), s32[]{:S(2)}) async-start(), calls=%async_computation.2 | async-start | bytes 4325376 | tf_op jit(solution)/shard_map/all_gather | solution.py:86
  10.8 265.7 %all-gather.11.cloned.1.call-start = ((), (), s32[]{:S(2)}) async-start(), calls=%async_computation.1 | async-start | bytes 3538944 | tf_op jit(solution)/shard_map/all_gather | solution.py:83
  42.1 119.3 %copy-start.1 = (bf16[384,4096]{1,0:T(8,128)(2,1)S(1)}, bf16[384,4096]{1,0:T(8,128)(2,1)}, u32[]{:S(2)}) copy-start(bf16[384,4096]{1,0:T(8,128)(2,1)} %all-gather.9.cloned.1.call-done) | copy-start | bytes 9437188
  161.4 14.8 %copy-start.6 = (f32[2,3,3,512]{3,0,2,1:T(2,128)S(1)}, f32[2,3,3,512]{3,0,2,1:T(2,128)}, u32[]{:S(2)}) copy-start(f32[2,3,3,512]{3,0,2,1:T(2,128)} %param.10) | copy-start | bytes 110596
  169.7 7.8 %collective-permute-start = (bf16[3,2,512]{2,1,0:T(2,128)(2,1)S(1)}, bf16[3,2,512]{2,1,0:T(2,128)(2,1)S(1)}, u32[]{:S(2)}, u32[]{:S(2)}) collective-permute-start(bf16[3,2,512]{2,1,0:T(2,128)(2,1)S(1)} %slice.436), channel_id=1, source_target_pairs={{0,8},{8,16},{16,24},{24,32},{32,40},{40,48},{48,56},{56,64},{64,7... | collective-permute-start | bytes 18440 | tf_op jit(solution)/shard_map/ppermute | solution.py:10
  177.8 6.8 %copy-start.11 = (f32[32,7]{0,1:T(8,128)S(1)}, f32[32,7]{0,1:T(8,128)}, u32[]{:S(2)}) copy-start(f32[32,7]{0,1:T(8,128)} %param.11) | copy-start | bytes 2692
  178.3 7.7 %collective-permute-start.1 = (bf16[6,512]{1,0:T(8,128)(2,1)S(1)}, bf16[6,512]{1,0:T(8,128)(2,1)S(1)}, u32[]{:S(2)}, u32[]{:S(2)}) collective-permute-start(bf16[6,512]{1,0:T(8,128)(2,1)S(1)} %slice.450), channel_id=1, source_target_pairs={{0,8},{8,16},{16,24},{24,32},{32,40},{40,48},{48,56},{56,64},{64,7... | collective-permute-start | bytes 18440 | tf_op jit(solution)/shard_map/ppermute | solution.py:10
  186.1 90.3 %copy-start.4 = (bf16[384,512]{1,0:T(8,128)(2,1)S(1)}, bf16[384,512]{1,0:T(8,128)(2,1)}, u32[]{:S(2)}) copy-start(bf16[384,512]{1,0:T(8,128)(2,1)} %param.7) | copy-start | bytes 1179652
  187.8 124.9 %all-gather.15.cloned.1.call-start = ((), (), s32[]{:S(2)}) async-start(), calls=%async_computation.3 | async-start | bytes 3538944 | tf_op jit(solution)/shard_map/all_gather | solution.py:40
  282.2 149.6 %all-gather.19.cloned.1.call-start = ((), (), s32[]{:S(2)}) async-start(), calls=%async_computation.5 | async-start | bytes 12976128 | tf_op jit(solution)/shard_map/all_gather | solution.py:50
  312.7 119.1 %copy-start.2 = (bf16[384,4096]{1,0:T(8,128)(2,1)S(1)}, bf16[384,4096]{1,0:T(8,128)(2,1)}, u32[]{:S(2)}) copy-start(bf16[384,4096]{1,0:T(8,128)(2,1)} %all-gather.15.cloned.1.call-done) | copy-start | bytes 9437188
  440.1 7.8 %collective-permute-start.2 = (bf16[3,2,512]{2,1,0:T(2,128)(2,1)S(1)}, bf16[3,2,512]{2,1,0:T(2,128)(2,1)S(1)}, u32[]{:S(2)}, u32[]{:S(2)}) collective-permute-start(bf16[3,2,512]{2,1,0:T(2,128)(2,1)S(1)} %slice.458), channel_id=1, source_target_pairs={{0,8},{8,16},{16,24},{24,32},{32,40},{40,48},{48,56},{56,64},{64,7... | collective-permute-start | bytes 18440 | tf_op jit(solution)/shard_map/ppermute | solution.py:10
  448.2 7.7 %copy-start.7 = (f32[32,128]{1,0:T(8,128)S(1)}, f32[32,128]{1,0:T(8,128)}, u32[]{:S(2)}) copy-start(f32[32,128]{1,0:T(8,128)} %param.12) | copy-start | bytes 49156
  448.8 131.7 %collective-permute-start.3 = (bf16[127,512]{1,0:T(8,128)(2,1)S(1)}, bf16[127,512]{1,0:T(8,128)(2,1)}, u32[]{:S(2)}, u32[]{:S(2)}) collective-permute-start(bf16[127,512]{1,0:T(8,128)(2,1)S(1)} %slice.472), channel_id=1, source_target_pairs={{0,8},{8,16},{16,24},{24,32},{32,40},{40,48},{48,56},{56,64},{64,7... | collective-permute-start | bytes 390152 | tf_op jit(solution)/shard_map/ppermute | solution.py:10
  577.5 6.9 %copy-start.5 = (pred[128,128]{1,0:T(8,128)(4,1)S(1)}, pred[128,128]{1,0:T(8,128)(4,1)}, u32[]{:S(2)}) copy-start(pred[128,128]{1,0:T(8,128)(4,1)} %fusion.115) | copy-start | bytes 49156
  584.4 3.0 copy-start
  584.4 3.0 copy-start.3
  589.1 0.8 copy-start.8
  589.1 0.8 copy-start.9
  589.1 0.8 copy-start.10
Sparse Core Ops, SparseCore 0:
  9.8 32.2 all-gather.8
  45.3 116.0 all-gather.16
  164.0 79.5 all-gather.12
  245.8 30.5 all-gather.10
  282.3 30.3 all-gather.14
  315.7 116.0 all-gather.18
where the time goes:
time: 598 us
  waiting for transfers between devices  386 us (65%)
  local copies, waits for them, and re-layouts  132 us (22%)
  matrix products  26.9 us (4%)
  starting transfers between devices  26 us (4%)
  between operations  14.4 us (2%)
  other arithmetic  12.3 us (2%)
    all_gather x2, waiting for transfers between devices, project(): lax.all_gather(weights, 'seq', axis=1, tiled=True)  233 us
    gather x2, local copies, waits for them, and re-layouts, toeplitz_conv(): current = jnp.where(lag >= 0, filt[:, jnp.clip(lag, 0, width - 1)], 0.0)  61.2 us
    all_gather x2, waiting for transfers between devices, normalized(): full = lax.all_gather(stream_loc, 'mp', axis=1, tiled=True)  60.3 us
    gather x2, local copies, waits for them, and re-layouts, toeplitz_conv(): filt[:, jnp.clip(lag + width, 0, width - 1)]  60.3 us
    all_gather x1, waiting for transfers between devices, local(): lax.all_gather(out_weight, 'seq', axis=0, tiled=True)  55.7 us
    all_gather x1, waiting for transfers between devices, local(): first_full = lax.all_gather(first, 'mp', axis=1, tiled=True)  32.9 us
    ppermute x4, starting transfers between devices, shifted(): return lax.ppermute(x, axis, pairs)  25.8 us
    dot_general x2, matrix products, project(): jnp.einsum('rd,cdf->crf', normed, lax.all_gather(weights, 'seq', axis=1,...  16.5 us
  transfers between devices with their start and end apart: 10, of which 9 were waited for; matrix products, arithmetic and copies ran while one was open for 24% of the time, Pallas kernels for 0%

commit v1 on v0

--- a/solution.py
+++ b/solution.py
@@ -83,7 +83,12 @@
     first_full = lax.all_gather(first, "mp", axis=1, tiled=True)
     delta = jnp.dot(
         first_full,
-        lax.all_gather(out_weight, "seq", axis=0, tiled=True),
+        jnp.concatenate(
+            lax.all_to_all(
+                jnp.stack([out_weight for _ in range(lax.axis_size("seq"))]), "seq", 0, 0
+            ),
+            0,
+        ),
         preferred_element_type=jnp.float32,
     )
     stream = (tokens.astype(jnp.float32) + delta).astype(jnp.bfloat16)

time: 598 us -> 577 us (0.965)
  waiting for transfers between devices: 386 us -> 352 us
  starting transfers between devices: 26 us -> 36.8 us
    all_gather x1 -> x0, waiting for transfers between devices: 55.7 us -> none  [local(): lax.all_gather(out_weight, 'seq', axis=0, tiled=True)]
    all_gather x2, waiting for transfers between devices: 233 us -> 268 us  [project(): lax.all_gather(weights, 'seq', axis=1, tiled=True)]
    all_gather x2, waiting for transfers between devices: 60.3 us -> 47.8 us  [normalized(): full = lax.all_gather(stream_loc, 'mp', axis=1, tiled=True)]
    all_to_all x0 -> x1, starting transfers between devices: none -> 10.8 us  [local(): lax.all_to_all(jnp.stack([out_weight for _ in range(lax.axis_size('seq'))...]
  transfers between devices with their start and end apart: 10 -> 10, of which waited for: 9 -> 8; matrix products, arithmetic and copies ran while one was open for 24% -> 26% of each run, Pallas kernels for 0% -> 0%
where the time goes in v1:
time: 577 us
  waiting for transfers between devices  352 us (61%)
  local copies, waits for them, and re-layouts  135 us (23%)
  starting transfers between devices  36.8 us (6%)
  matrix products  26.9 us (5%)
  between operations  14.1 us (2%)
  other arithmetic  12.3 us (2%)
    all_gather x2, waiting for transfers between devices, project(): lax.all_gather(weights, 'seq', axis=1, tiled=True)  268 us
    gather x2, local copies, waits for them, and re-layouts, toeplitz_conv(): current = jnp.where(lag >= 0, filt[:, jnp.clip(lag, 0, width - 1)], 0.0)  61.2 us
    gather x2, local copies, waits for them, and re-layouts, toeplitz_conv(): filt[:, jnp.clip(lag + width, 0, width - 1)]  60.3 us
    all_gather x2, waiting for transfers between devices, normalized(): full = lax.all_gather(stream_loc, 'mp', axis=1, tiled=True)  47.8 us
    all_gather x1, waiting for transfers between devices, local(): first_full = lax.all_gather(first, 'mp', axis=1, tiled=True)  32.4 us
    ppermute x4, starting transfers between devices, shifted(): return lax.ppermute(x, axis, pairs)  25.8 us
    dot_general x2, matrix products, project(): jnp.einsum('rd,cdf->crf', normed, lax.all_gather(weights, 'seq', axis=1,...  16.5 us
  transfers between devices with their start and end apart: 10, of which 8 were waited for; matrix products, arithmetic and copies ran while one was open for 26% of the time, Pallas kernels for 0%

profile of v1, /device:TPU:88, one launch (start us, length us, event | category | flops | bytes accessed | tf_op | source)
XLA Modules:
  0.0 576.8 jit_solution(15837616374100387295)
XLA Ops:
  7.2 0.7 all-gather.8.cloned.1.call-update
  7.9 2.1 fusion.119
  10.0 3.3 stack.2
  13.4 10.8 %all-to-all-start = ((bf16[32,128,512]{2,1,0:T(8,128)(2,1)}), bf16[32,128,512]{2,1,0:T(8,128)(2,1)}, u32[]{:S(2)}, u32[]{:S(2)}) async-start(bf16[32,128,512]{2,1,0:T(8,128)(2,1)} %stack.2), calls=%async_computation | async-start | bytes 8388608 | tf_op jit(solution)/shard_map/all_to_all | solution.py:87
  24.2 17.9 %all-gather.8.cloned.1.call-done = bf16[384,4096]{1,0:T(8,128)(2,1)} async-done(((bf16[384,512]{1,0:T(8,128)(2,1)}), bf16[384,4096]{1,0:T(8,128)(2,1)}) %all-gather.8.cloned.1.call-update) | async-done | bytes 3145744 | tf_op jit(solution)/shard_map/all_gather | solution.py:40
  42.1 2.7 fusion.4
  44.9 151.9 %all-gather.14.cloned.1.call-done = bf16[1,3,4096,512]{3,2,1,0:T(8,128)(2,1)} async-done(((bf16[1,3,128,512]{3,2,1,0:T(8,128)(2,1)}), bf16[1,3,4096,512]{3,2,1,0:T(8,128)(2,1)}) %all-gather.14.cloned.1.call-update) | async-done | bytes 12582928 | tf_op jit(solution)/shard_map/all_gather | solution.py:50
  196.8 8.3 %fusion.39 = bf16[3,384,512]{2,1,0:T(8,128)(2,1)S(1)} fusion(bf16[1,3,4096,512]{3,2,1,0:T(8,128)(2,1)} %all-gather.14.cloned.1.call-done, bf16[384,4096]{1,0:T(8,128)(2,1)S(1)} %copy-done.1, f32[4096]{0:T(1024)S(1)} %bitcast.256, f32[384]{0:T(512)S(1)} %add_rsqrt_fusion.1), kind=kOutput, calls=%fused_computation.35 | convolution fusion | flops 4838719488 | bytes 16926208 | tf_op jit(solution)/shard_map/rd,cdf->crf/dot_general | solution.py:47
  205.1 6.5 %collective-permute-start = (bf16[3,2,512]{2,1,0:T(2,128)(2,1)S(1)}, bf16[3,2,512]{2,1,0:T(2,128)(2,1)S(1)}, u32[]{:S(2)}, u32[]{:S(2)}) collective-permute-start(bf16[3,2,512]{2,1,0:T(2,128)(2,1)S(1)} %slice.436), channel_id=1, source_target_pairs={{0,8},{8,16},{16,24},{24,32},{32,40},{40,48},{48,56},{56,64},{64,7... | collective-permute-start | bytes 18440 | tf_op jit(solution)/shard_map/ppermute | solution.py:10
  211.6 0.6 fusion.120
  212.2 0.7 collective-permute-done
  212.9 0.3 fusion.106
  213.2 0.5 fusion.85
  213.7 6.3 %collective-permute-start.1 = (bf16[6,512]{1,0:T(8,128)(2,1)S(1)}, bf16[6,512]{1,0:T(8,128)(2,1)S(1)}, u32[]{:S(2)}, u32[]{:S(2)}) collective-permute-start(bf16[6,512]{1,0:T(8,128)(2,1)S(1)} %slice.450), channel_id=1, source_target_pairs={{0,8},{8,16},{16,24},{24,32},{32,40},{40,48},{48,56},{56,64},{64,7... | collective-permute-start | bytes 18440 | tf_op jit(solution)/shard_map/ppermute | solution.py:10
  220.3 0.1 broadcast_in_dim.53
  220.5 0.1 broadcast_in_dim.55
  220.6 0.1 broadcast_in_dim.57
  221.1 0.3 collective-permute-done.1
  221.4 0.1 maximum_convert_fusion
  221.5 1.7 fusion.76
  223.3 32.4 %all-gather.10.cloned.1.call-done = bf16[384,4096]{1,0:T(8,128)(2,1)} async-done(((bf16[384,512]{1,0:T(8,128)(2,1)}), bf16[384,4096]{1,0:T(8,128)(2,1)}) %all-gather.10.cloned.1.call-update) | async-done | bytes 3145744 | tf_op jit(solution)/shard_map/all_gather | solution.py:83
  255.7 5.7 fusion.50
  261.5 0.5 all-gather.16.cloned.1.call-update
  262.0 29.9 %all-gather.12.cloned.1.call-done = bf16[384,4096]{1,0:T(8,128)(2,1)} async-done(((bf16[384,512]{1,0:T(8,128)(2,1)}), bf16[384,4096]{1,0:T(8,128)(2,1)}) %all-gather.12.cloned.1.call-update) | async-done | bytes 3145744 | tf_op jit(solution)/shard_map/all_gather | solution.py:40
  291.9 2.7 fusion.7
  294.7 116.4 %all-gather.16.cloned.1.call-done = bf16[1,3,4096,512]{3,2,1,0:T(8,128)(2,1)} async-done(((bf16[1,3,128,512]{3,2,1,0:T(8,128)(2,1)}), bf16[1,3,4096,512]{3,2,1,0:T(8,128)(2,1)}) %all-gather.16.cloned.1.call-update) | async-done | bytes 12582928 | tf_op jit(solution)/shard_map/all_gather | solution.py:50
  411.1 8.2 %fusion.34 = bf16[3,384,512]{2,1,0:T(8,128)(2,1)S(1)} fusion(bf16[1,3,4096,512]{3,2,1,0:T(8,128)(2,1)} %all-gather.16.cloned.1.call-done, bf16[384,4096]{1,0:T(8,128)(2,1)S(1)} %copy-done.2, f32[4096]{0:T(1024)S(1)} %bitcast.255, f32[384]{0:T(512)S(1)} %add_rsqrt_fusion), kind=kOutput, calls=%fused_computation.34 | convolution fusion | flops 4838719488 | bytes 16926208 | tf_op jit(solution)/shard_map/rd,cdf->crf/dot_general | solution.py:47
  419.3 6.5 %collective-permute-start.2 = (bf16[3,2,512]{2,1,0:T(2,128)(2,1)S(1)}, bf16[3,2,512]{2,1,0:T(2,128)(2,1)S(1)}, u32[]{:S(2)}, u32[]{:S(2)}) collective-permute-start(bf16[3,2,512]{2,1,0:T(2,128)(2,1)S(1)} %slice.458), channel_id=1, source_target_pairs={{0,8},{8,16},{16,24},{24,32},{32,40},{40,48},{48,56},{56,64},{64,7... | collective-permute-start | bytes 18440 | tf_op jit(solution)/shard_map/ppermute | solution.py:10
  425.9 1.3 collective-permute-done.2
  427.2 0.3 fusion.102
  427.5 0.5 fusion.58
  428.0 6.5 %collective-permute-start.3 = (bf16[127,512]{1,0:T(8,128)(2,1)S(1)}, bf16[127,512]{1,0:T(8,128)(2,1)}, u32[]{:S(2)}, u32[]{:S(2)}) collective-permute-start(bf16[127,512]{1,0:T(8,128)(2,1)S(1)} %slice.472), channel_id=1, source_target_pairs={{0,8},{8,16},{16,24},{24,32},{32,40},{40,48},{48,56},{56,64},{64,7... | collective-permute-start | bytes 390152 | tf_op jit(solution)/shard_map/ppermute | solution.py:10
  434.5 0.6 fusion.115
  435.1 0.1 copy.17
  435.2 54.8 %gather_fusion.1 = f32[16384,32]{1,0:T(8,128)} fusion(f32[32,128]{0,1:T(8,128)S(1)} %copy.17, s32[16384]{0:T(1024)S(1)} %fusion.114), kind=kCustom, calls=%fused_computation.1 | custom fusion | bytes 4259840 | tf_op jit(solution)/shard_map/gather | solution.py:33
  490.0 5.5 copy.22
  495.5 54.8 %gather_fusion = f32[16384,32]{1,0:T(8,128)} fusion(f32[32,128]{0,1:T(8,128)S(1)} %copy.17, s32[16384]{0:T(1024)S(1)} %fusion.112), kind=kCustom, calls=%fused_computation | custom fusion | bytes 4259840 | tf_op jit(solution)/shard_map/gather | solution.py:32
  550.3 6.4 %copy.18 = f32[128,128,32]{1,0,2:T(8,128)} copy(f32[128,128,32]{2,1,0:T(8,128)} %bitcast.251) | data formatting | bytes 4194304 | tf_op jit(solution)/shard_map/gather | solution.py:32
  556.8 0.9 copy.16
  557.7 2.0 slice.428
  559.7 1.8 pad_maximum_fusion.2
  561.5 1.2 copy.20
  562.7 0.9 slice.431
  563.7 2.9 fusion.18
  566.6 1.8 fusion.47
  568.4 0.4 copy.24
  568.9 0.3 copy.25
  569.2 1.0 fusion.70
  (60 shorter events, 1.4 us)
Async XLA Ops:
  7.2 35.0 %all-gather.8.cloned.1.call-start = ((), (), s32[]{:S(2)}) async-start(), calls=%async_computation.1 | async-start | bytes 3538944 | tf_op jit(solution)/shard_map/all_gather | solution.py:40
  7.9 188.9 %all-gather.14.cloned.1.call-start = ((), (), s32[]{:S(2)}) async-start(), calls=%async_computation.4 | async-start | bytes 12976128 | tf_op jit(solution)/shard_map/all_gather | solution.py:50
  13.4 10.8 %copy-start.7 = (f32[2,4096]{1,0:T(2,128)S(1)}, f32[2,4096]{1,0:T(2,128)}, u32[]{:S(2)}) copy-start(f32[2,4096]{1,0:T(2,128)} %param.8) | copy-start | bytes 98308
  13.4 209.9 %all-to-all-start = ((bf16[32,128,512]{2,1,0:T(8,128)(2,1)}), bf16[32,128,512]{2,1,0:T(8,128)(2,1)}, u32[]{:S(2)}, u32[]{:S(2)}) async-start(bf16[32,128,512]{2,1,0:T(8,128)(2,1)} %stack.2), calls=%async_computation | async-start | bytes 8388608 | tf_op jit(solution)/shard_map/all_to_all | solution.py:87
  24.1 231.6 %all-gather.10.cloned.1.call-start = ((), (), s32[]{:S(2)}) async-start(), calls=%async_computation.2 | async-start | bytes 3538944 | tf_op jit(solution)/shard_map/all_gather | solution.py:83
  42.1 154.7 %copy-start.1 = (bf16[384,4096]{1,0:T(8,128)(2,1)S(1)}, bf16[384,4096]{1,0:T(8,128)(2,1)}, u32[]{:S(2)}) copy-start(bf16[384,4096]{1,0:T(8,128)(2,1)} %all-gather.8.cloned.1.call-done) | copy-start | bytes 9437188
  196.8 14.8 %copy-start.6 = (f32[2,3,3,512]{3,0,2,1:T(2,128)S(1)}, f32[2,3,3,512]{3,0,2,1:T(2,128)}, u32[]{:S(2)}) copy-start(f32[2,3,3,512]{3,0,2,1:T(2,128)} %param.10) | copy-start | bytes 110596
  205.1 7.8 %collective-permute-start = (bf16[3,2,512]{2,1,0:T(2,128)(2,1)S(1)}, bf16[3,2,512]{2,1,0:T(2,128)(2,1)S(1)}, u32[]{:S(2)}, u32[]{:S(2)}) collective-permute-start(bf16[3,2,512]{2,1,0:T(2,128)(2,1)S(1)} %slice.436), channel_id=1, source_target_pairs={{0,8},{8,16},{16,24},{24,32},{32,40},{40,48},{48,56},{56,64},{64,7... | collective-permute-start | bytes 18440 | tf_op jit(solution)/shard_map/ppermute | solution.py:10
  213.2 6.8 %copy-start.12 = (f32[32,7]{0,1:T(8,128)S(1)}, f32[32,7]{0,1:T(8,128)}, u32[]{:S(2)}) copy-start(f32[32,7]{0,1:T(8,128)} %param.11) | copy-start | bytes 2692
  213.7 7.7 %collective-permute-start.1 = (bf16[6,512]{1,0:T(8,128)(2,1)S(1)}, bf16[6,512]{1,0:T(8,128)(2,1)S(1)}, u32[]{:S(2)}, u32[]{:S(2)}) collective-permute-start(bf16[6,512]{1,0:T(8,128)(2,1)S(1)} %slice.450), channel_id=1, source_target_pairs={{0,8},{8,16},{16,24},{24,32},{32,40},{40,48},{48,56},{56,64},{64,7... | collective-permute-start | bytes 18440 | tf_op jit(solution)/shard_map/ppermute | solution.py:10
  221.5 34.2 %copy-start.4 = (bf16[384,512]{1,0:T(8,128)(2,1)S(1)}, bf16[384,512]{1,0:T(8,128)(2,1)}, u32[]{:S(2)}) copy-start(bf16[384,512]{1,0:T(8,128)(2,1)} %param.7) | copy-start | bytes 1179652
  223.2 68.7 %all-gather.12.cloned.1.call-start = ((), (), s32[]{:S(2)}) async-start(), calls=%async_computation.3 | async-start | bytes 3538944 | tf_op jit(solution)/shard_map/all_gather | solution.py:40
  261.4 149.6 %all-gather.16.cloned.1.call-start = ((), (), s32[]{:S(2)}) async-start(), calls=%async_computation.5 | async-start | bytes 12976128 | tf_op jit(solution)/shard_map/all_gather | solution.py:50
  291.9 119.1 %copy-start.2 = (bf16[384,4096]{1,0:T(8,128)(2,1)S(1)}, bf16[384,4096]{1,0:T(8,128)(2,1)}, u32[]{:S(2)}) copy-start(bf16[384,4096]{1,0:T(8,128)(2,1)} %all-gather.12.cloned.1.call-done) | copy-start | bytes 9437188
  419.3 7.8 %collective-permute-start.2 = (bf16[3,2,512]{2,1,0:T(2,128)(2,1)S(1)}, bf16[3,2,512]{2,1,0:T(2,128)(2,1)S(1)}, u32[]{:S(2)}, u32[]{:S(2)}) collective-permute-start(bf16[3,2,512]{2,1,0:T(2,128)(2,1)S(1)} %slice.458), channel_id=1, source_target_pairs={{0,8},{8,16},{16,24},{24,32},{32,40},{40,48},{48,56},{56,64},{64,7... | collective-permute-start | bytes 18440 | tf_op jit(solution)/shard_map/ppermute | solution.py:10
  427.5 7.7 %copy-start.8 = (f32[32,128]{1,0:T(8,128)S(1)}, f32[32,128]{1,0:T(8,128)}, u32[]{:S(2)}) copy-start(f32[32,128]{1,0:T(8,128)} %param.12) | copy-start | bytes 49156
  428.0 131.7 %collective-permute-start.3 = (bf16[127,512]{1,0:T(8,128)(2,1)S(1)}, bf16[127,512]{1,0:T(8,128)(2,1)}, u32[]{:S(2)}, u32[]{:S(2)}) collective-permute-start(bf16[127,512]{1,0:T(8,128)(2,1)S(1)} %slice.472), channel_id=1, source_target_pairs={{0,8},{8,16},{16,24},{24,32},{32,40},{40,48},{48,56},{56,64},{64,7... | collective-permute-start | bytes 390152 | tf_op jit(solution)/shard_map/ppermute | solution.py:10
  556.7 6.9 %copy-start.5 = (pred[128,128]{1,0:T(8,128)(4,1)S(1)}, pred[128,128]{1,0:T(8,128)(4,1)}, u32[]{:S(2)}) copy-start(pred[128,128]{1,0:T(8,128)(4,1)} %fusion.115) | copy-start | bytes 49156
  563.6 3.0 copy-start
  563.6 3.0 copy-start.3
  568.4 0.8 copy-start.9
  568.4 0.8 copy-start.10
  568.4 0.8 copy-start.11
Sparse Core Ops, SparseCore 0:
  9.8 32.2 all-gather.7
  45.3 151.4 all-gather.13
  223.3 32.3 all-gather.9
  261.5 30.3 all-gather.11
  294.9 116.0 all-gather.15
